TPU v7x, 32 devices: a whole 2x2x4 slice. The times are simulated.
32 devices in a mesh: dp: 2 (over x), row: 4 (over y, core), col: 4 (over z).
Axes of the slice: x: 2, y: 2, z: 4, core: 2. Of those that a mesh axis runs over, the one named last changes fastest.
Arguments:
- tokens: bfloat16 [5120, 2048], P(('dp', 'col'), 'row'), may hold values from -6 to 6
- cotangent: bfloat16 [5120, 2048], P(('dp', 'col'), 'row'), may hold values from -6 to 6
- seg_ids: int32 [5120], P('dp'), may hold values from 0 to 12, as said below
- positions: int32 [5120], P('dp'), may hold values from 0 to 1279, as said below
- parents: int32 [2, 13], P('dp'), may hold values from 0 to 4, as said below
- tree_sets: int32 [2], P('dp'), may hold values from 0 to 7
- gain_q: float32 [2048], P('col'), may hold values from 0.25 to 1.75
- gain_k: float32 [2048], P('col'), may hold values from 0.25 to 1.75
- gain_attn: float32 [2048], P('row'), may hold values from 0.25 to 1.75
- gain_ffn: float32 [2048], P('row'), may hold values from 0.25 to 1.75
- query_key_value_weight: bfloat16 [2048, 3, 2048], P('row', None, 'col'), may hold values from -0.125 to 0.125
- output_weight: bfloat16 [2048, 2048], P('col', 'row'), may hold values from -0.125 to 0.125
- gate_up_weight: bfloat16 [2048, 2, 8192], P('row', None, 'col'), may hold values from -0.125 to 0.125
- down_weight: bfloat16 [8192, 2048], P('col', 'row'), may hold values from -0.0625 to 0.0625
- query_key_value_adapter_first: float32 [3, 8, 16, 2048], P(None, None, None, 'row'), may hold values from -0.125 to 0.125
- query_key_value_adapter_second: float32 [3, 8, 16, 2048], P(None, None, None, 'col'), may hold values from -0.5 to 0.5
- output_adapter_first: float32 [8, 16, 2048], P(None, None, 'col'), may hold values from -0.125 to 0.125
- output_adapter_second: float32 [8, 16, 2048], P(None, None, 'row'), may hold values from -0.5 to 0.5
- gate_up_adapter_first: float32 [2, 8, 16, 2048], P(None, None, None, 'row'), may hold values from -0.125 to 0.125
- gate_up_adapter_second: float32 [2, 8, 16, 8192], P(None, None, None, 'col'), may hold values from -0.5 to 0.5
- down_adapter_first: float32 [8, 16, 8192], P(None, None, 'col'), may hold values from -0.0625 to 0.0625
- down_adapter_second: float32 [8, 16, 2048], P(None, None, 'row'), may hold values from -0.5 to 0.5
Outputs:
- layer_out: bfloat16 [5120, 2048], P(('dp', 'col'), 'row')
- input_grad: float32 [5120, 2048], P(('dp', 'col'), 'row')
- grad_a_qkv: float32 [3, 8, 16, 2048], P(None, 'dp', 'col', 'row')
- grad_b_qkv: float32 [3, 8, 16, 2048], P(None, 'dp', 'row', 'col')
- grad_a_out: float32 [8, 16, 2048], P('dp', 'row', 'col')
- grad_b_out: float32 [8, 16, 2048], P('dp', 'col', 'row')
- grad_a_gu: float32 [2, 8, 16, 2048], P(None, 'dp', 'col', 'row')
- grad_b_gu: float32 [2, 8, 16, 8192], P(None, 'dp', 'row', 'col')
- grad_a_down: float32 [8, 16, 8192], P('dp', 'row', 'col')
- grad_b_down: float32 [8, 16, 2048], P('dp', 'col', 'row')
Inputs may be any that keep to these rules, and one draw needn't show every extreme that they name: `seg_ids`: in each tree the first 1024 tokens are segment 0, the trunk; the other 12 segments of 128 tokens each follow in any order: branches are 1 to 4, leaves the higher numbers. The trunk's tokens have positions 0 to 1023 in order, a branch's 1024 onward, a leaf's 1024 + 128 onward. `parents`: the trunk and the branches have parent 0; each leaf has a branch as parent, and each branch has 2 leaves.
All inputs are finite; a program needn't handle non-finite values.
Results may differ from a plain program's by a relative error of at most 0.025.
Values may be sent and summed in bfloat16 or wider, within the bound.
A program may use at most 320 MiB of HBM per device.

v0:
```python
import jax
import jax.numpy as jnp
from jax import lax
from jax.sharding import PartitionSpec as P

D = 2048
HEAD = 128
RANK = 16
epsilon = 1e-06
rope_base = 500000.0
masked_out = -1e30
low = jnp.bfloat16
wide = jnp.float32
last_last = (((1,), (1,)), ((), ()))
first_first = (((0,), (0,)), ((), ()))


def dot(left, right):
    return jnp.dot(left, right, preferred_element_type=wide)


def dot_t(left, right):
    return lax.dot_general(left, right, last_last, preferred_element_type=wide)


def t_dot(left, right):
    return lax.dot_general(left, right, first_first, preferred_element_type=wide)


def angles(positions):
    half_width = HEAD // 2
    frequency = rope_base ** (-(jnp.arange(half_width, dtype=wide) * 2.0) / HEAD)
    angle_table = positions.astype(wide)[:, None] * frequency[None, :]
    return (jnp.cos(angle_table)[:, None, :], jnp.sin(angle_table)[:, None, :])


def rotate(values, cosine, sine):
    half_width = values.shape[-1] // 2
    first_half = values[..., :half_width]
    second_half = values[..., half_width:]
    return jnp.concatenate(
        [first_half * cosine - second_half * sine, second_half * cosine + first_half * sine],
        axis=-1,
    )


def norm_factor(square_sum):
    return lax.rsqrt(square_sum / D + epsilon)


def norm_back(scaled, flat, factor, cross_sum):
    return factor[:, None] * (scaled - flat * (cross_sum / D)[:, None])


def tree_mask(seg_ids, positions, parents):
    parent_row = parents[0]
    labels = jnp.arange(parent_row.shape[0], dtype=jnp.int32)
    parent_tok = jnp.sum(
        jnp.where(seg_ids[:, None] == labels[None, :], parent_row[None, :], 0), axis=1
    )
    grand_tok = jnp.sum(
        jnp.where(parent_tok[:, None] == labels[None, :], parent_row[None, :], 0), axis=1
    )
    on_path = (
        (seg_ids[None, :] == seg_ids[:, None])
        | (seg_ids[None, :] == parent_tok[:, None])
        | (seg_ids[None, :] == grand_tok[:, None])
    )
    return on_path & (positions[None, :] <= positions[:, None])


def per_device(
    tokens,
    cotangent,
    seg_ids,
    positions,
    parents,
    tree_sets,
    gain_q,
    gain_k,
    gain_attn,
    gain_ffn,
    query_key_value_weight,
    output_weight,
    gate_up_weight,
    down_weight,
    query_key_value_adapter_first,
    query_key_value_adapter_second,
    output_adapter_first,
    output_adapter_second,
    gate_up_adapter_first,
    gate_up_adapter_second,
    down_adapter_first,
    down_adapter_second,
):
    dp_count = lax.axis_size("dp")
    row_count = lax.axis_size("row")
    col_count = lax.axis_size("col")
    row_at = lax.axis_index("row")
    tree_tokens = seg_ids.shape[0]
    assert tree_sets.shape[0] == 1
    set_count = output_adapter_first.shape[0]
    own = tokens.shape[0] // row_count
    group = own * col_count
    width_row = tokens.shape[1]
    width_col = gain_q.shape[0]
    hidden_col = down_weight.shape[0]
    heads_col = width_col // HEAD
    score_scale = HEAD ** (-0.5)
    tree_set = tree_sets[0]

    def pick(table, axis):
        return lax.dynamic_index_in_dim(table, tree_set, axis, keepdims=False)

    narrow = jnp.concatenate(
        [
            pick(query_key_value_adapter_first, 1),
            pick(gate_up_adapter_first, 1),
            pick(output_adapter_second, 0)[None],
            pick(down_adapter_second, 0)[None],
        ],
        axis=0,
    ).astype(low)
    narrow_all = lax.all_gather(narrow, "row", axis=2, tiled=True)
    a_qkv = narrow_all[:3].reshape(3 * RANK, D)
    a_gu = narrow_all[3:5].reshape(2 * RANK, D)
    b_out = narrow_all[5]
    b_down = narrow_all[6]
    b_qkv = pick(query_key_value_adapter_second, 1).astype(low)
    b_gu = pick(gate_up_adapter_second, 1).astype(low)
    a_out = pick(output_adapter_first, 0).astype(low)
    a_down = pick(down_adapter_first, 0).astype(low)
    gains = lax.all_gather(jnp.stack([gain_attn, gain_ffn]), "row", axis=1, tiled=True)
    w_qkv = lax.all_gather(query_key_value_weight, "row", axis=0, tiled=True).reshape(
        D, 3 * width_col
    )
    w_out = lax.all_gather(output_weight, "row", axis=1, tiled=True)
    w_gu = lax.all_gather(gate_up_weight, "row", axis=0, tiled=True).reshape(D, 2 * hidden_col)
    w_down = lax.all_gather(down_weight, "row", axis=1, tiled=True)

    def to_tokens(values):
        return lax.all_to_all(values, "row", split_axis=0, concat_axis=1, tiled=True)

    def to_width(values):
        return lax.all_to_all(values, "row", split_axis=1, concat_axis=0, tiled=True)

    def gather_col(values):
        return lax.all_gather(values, "col", axis=0, tiled=True)

    def scatter_col(values):
        return lax.psum_scatter(values.astype(low), "col", scatter_dimension=0, tiled=True).astype(
            wide
        )

    def to_heads(values, parts):
        by_head = (
            values.reshape(group, parts, heads_col, HEAD)
            .transpose(2, 0, 1, 3)
            .reshape(heads_col, group, parts * HEAD)
        )
        moved = lax.all_to_all(by_head, "row", split_axis=0, concat_axis=0, tiled=True)
        return (
            moved.reshape(row_count, col_count, own, parts * HEAD)
            .transpose(1, 0, 2, 3)
            .reshape(tree_tokens, parts * HEAD)
        )

    def from_heads(values, parts):
        by_row = (
            values.reshape(col_count, row_count, own, parts * HEAD)
            .transpose(1, 0, 2, 3)
            .reshape(row_count, group, parts * HEAD)
        )
        moved = lax.all_to_all(by_row, "row", split_axis=0, concat_axis=0, tiled=True)
        return (
            moved.reshape(heads_col, group, parts, HEAD)
            .transpose(1, 2, 0, 3)
            .reshape(group, parts * width_col)
        )

    x_own = to_tokens(tokens)
    x = gather_col(x_own)
    red_qkv = dot_t(x, a_qkv).astype(low)
    raw = dot(x, w_qkv)
    extra = jnp.concatenate(
        [dot(red_qkv[:, RANK * j : RANK * (j + 1)], b_qkv[j]) for j in range(3)], axis=1
    )
    raw = raw + extra
    q_raw = raw[:, :width_col]
    k_raw = raw[:, width_col : 2 * width_col]
    v_raw = raw[:, 2 * width_col :]
    square_qk = lax.psum(
        jnp.stack([jnp.sum(q_raw * q_raw, axis=1), jnp.sum(k_raw * k_raw, axis=1)]), "col"
    )
    q_factor = norm_factor(square_qk[0])
    k_factor = norm_factor(square_qk[1])
    q_flat = q_raw * q_factor[:, None]
    k_flat = k_raw * k_factor[:, None]
    pos_own = lax.dynamic_index_in_dim(
        positions.reshape(col_count, row_count, own), row_at, 1, keepdims=False
    ).reshape(group)
    cos_own, sin_own = angles(pos_own)

    def turn(values, sine):
        return rotate(values.reshape(group, heads_col, HEAD), cos_own, sine).reshape(
            group, width_col
        )

    q_low = turn(q_flat * gain_q, sin_own).astype(low)
    k_low = turn(k_flat * gain_k, sin_own).astype(low)
    qkv_head = to_heads(jnp.concatenate([q_low, k_low, v_raw.astype(low)], axis=1), 3)
    q_head = qkv_head[:, :HEAD]
    k_head = qkv_head[:, HEAD : 2 * HEAD]
    v_head = qkv_head[:, 2 * HEAD :]
    visible = tree_mask(seg_ids, positions, parents)
    scores = jnp.where(visible, dot_t(q_head, k_head) * score_scale, masked_out)
    highest = jnp.max(scores, axis=1, keepdims=True)
    raised = jnp.exp(scores - highest)
    probs = raised / jnp.sum(raised, axis=1, keepdims=True)
    probs_low = probs.astype(low)
    attn_head = dot(probs_low, v_head).astype(low)
    attn = from_heads(attn_head, 1)
    red_out = dot_t(attn, a_out).astype(low)
    a_raw = scatter_col(dot(attn, w_out) + dot(red_out, b_out))
    a_factor = norm_factor(jnp.sum(a_raw * a_raw, axis=1))
    a_flat = a_raw * a_factor[:, None]
    h_own = x_own.astype(wide) + a_flat * gains[0]
    h = gather_col(h_own.astype(low))
    red_gu = dot_t(h, a_gu).astype(low)
    gate = dot(h, w_gu[:, :hidden_col]) + dot(red_gu[:, :RANK], b_gu[0])
    up = dot(h, w_gu[:, hidden_col:]) + dot(red_gu[:, RANK:], b_gu[1])
    sigma = jax.nn.sigmoid(gate)
    hidden = (gate * sigma * up).astype(low)
    red_down = dot_t(hidden, a_down).astype(low)
    f_raw = scatter_col(dot(hidden, w_down) + dot(red_down, b_down))
    f_factor = norm_factor(jnp.sum(f_raw * f_raw, axis=1))
    f_flat = f_raw * f_factor[:, None]
    out_own = (h_own + f_flat * gains[1]).astype(low)
    layer_out = to_width(out_own)
    g_own = to_tokens(cotangent).astype(wide)
    scaled_f = g_own * gains[1]
    d_f_own = norm_back(scaled_f, f_flat, f_factor, jnp.sum(scaled_f * f_flat, axis=1)).astype(low)
    d_f = gather_col(d_f_own)
    back_down = dot_t(d_f, b_down).astype(low)
    d_hidden = dot_t(d_f, w_down) + dot(back_down, a_down)
    d_gate = (d_hidden * up * sigma * (1.0 + gate * (1.0 - sigma))).astype(low)
    d_up = (d_hidden * (gate * sigma)).astype(low)
    back_gate = dot_t(d_gate, b_gu[0]).astype(low)
    back_up = dot_t(d_up, b_gu[1]).astype(low)
    back_gu = jnp.concatenate([back_gate, back_up], axis=1)
    d_h = g_own + scatter_col(
        dot_t(d_gate, w_gu[:, :hidden_col]) + dot_t(d_up, w_gu[:, hidden_col:]) + dot(back_gu, a_gu)
    )
    scaled_a = d_h * gains[0]
    d_a_own = norm_back(scaled_a, a_flat, a_factor, jnp.sum(scaled_a * a_flat, axis=1)).astype(low)
    d_a = gather_col(d_a_own)
    back_out = dot_t(d_a, b_out).astype(low)
    d_attn = (dot_t(d_a, w_out) + dot(back_out, a_out)).astype(low)
    d_attn_head = to_heads(d_attn, 1)
    d_probs = dot_t(d_attn_head, v_head)
    inner = jnp.sum(probs * d_probs, axis=1, keepdims=True)
    d_scores = (probs * (d_probs - inner)).astype(low)
    dq_head = (dot(d_scores, k_head) * score_scale).astype(low)
    dk_head = (t_dot(d_scores, q_head) * score_scale).astype(low)
    dv_head = t_dot(probs_low, d_attn_head).astype(low)
    d_qkv = from_heads(jnp.concatenate([dq_head, dk_head, dv_head], axis=1), 3)
    dq_n = turn(d_qkv[:, :width_col].astype(wide), -sin_own) * gain_q
    dk_n = turn(d_qkv[:, width_col : 2 * width_col].astype(wide), -sin_own) * gain_k
    cross_qk = lax.psum(
        jnp.stack([jnp.sum(dq_n * q_flat, axis=1), jnp.sum(dk_n * k_flat, axis=1)]), "col"
    )
    d_q = norm_back(dq_n, q_flat, q_factor, cross_qk[0]).astype(low)
    d_k = norm_back(dk_n, k_flat, k_factor, cross_qk[1]).astype(low)
    d_v = d_qkv[:, 2 * width_col :]
    d_raw = jnp.concatenate([d_q, d_k, d_v], axis=1)
    back_qkv = jnp.concatenate(
        [dot_t(d, b) for d, b in zip((d_q, d_k, d_v), (b_qkv[0], b_qkv[1], b_qkv[2]))], axis=1
    ).astype(low)
    in_own = d_h + scatter_col(dot_t(d_raw, w_qkv) + dot(back_qkv, a_qkv))
    input_grad = to_width(in_own.astype(low)).astype(wide)
    full_width = jnp.concatenate(
        [t_dot(back_qkv, x), t_dot(back_gu, h), t_dot(red_out, d_a), t_dot(red_down, d_f)], axis=0
    ).astype(low)
    full_width = lax.psum_scatter(full_width, "row", scatter_dimension=1, tiled=True)
    full_width = full_width.reshape(7, col_count, RANK // col_count, width_row).transpose(
        1, 0, 2, 3
    )
    full_width = lax.psum_scatter(full_width, "col", scatter_dimension=0, tiled=False)
    col_width = jnp.concatenate(
        [t_dot(red_qkv[:, RANK * j : RANK * (j + 1)], d) for j, d in enumerate((d_q, d_k, d_v))]
        + [
            t_dot(back_out, attn),
            t_dot(red_gu[:, :RANK], d_gate),
            t_dot(red_gu[:, RANK:], d_up),
            t_dot(back_down, hidden),
        ],
        axis=1,
    ).astype(low)
    col_width = lax.psum_scatter(col_width, "row", scatter_dimension=0, tiled=True)
    onehot = (tree_set == jnp.arange(set_count, dtype=jnp.int32)).astype(wide)
    owner = jnp.concatenate([full_width.reshape(-1), col_width.reshape(-1)])
    owner_all = lax.all_gather(owner, "dp", axis=0, tiled=False).astype(wide)
    onehot_all = lax.all_gather(onehot, "dp", axis=0, tiled=False)
    sets_own = set_count // dp_count
    onehot_own = lax.dynamic_slice_in_dim(onehot_all, lax.axis_index("dp") * sets_own, sets_own, 1)
    per_set = jnp.sum(onehot_own[:, :, None] * owner_all[:, None, :], axis=0)
    split_at = full_width.size
    full_sets = per_set[:, :split_at].reshape(sets_own, 7, RANK // col_count, width_row)
    col_sets = per_set[:, split_at:].reshape(sets_own, RANK // row_count, -1)
    grad_a_qkv = full_sets[:, :3].transpose(1, 0, 2, 3)
    grad_a_gu = full_sets[:, 3:5].transpose(1, 0, 2, 3)
    grad_b_out = full_sets[:, 5]
    grad_b_down = full_sets[:, 6]
    grad_b_qkv = jnp.stack([col_sets[..., width_col * j : width_col * (j + 1)] for j in range(3)])
    grad_a_out = col_sets[..., 3 * width_col : 4 * width_col]
    gu_at = 4 * width_col
    grad_b_gu = jnp.stack(
        [col_sets[..., gu_at + hidden_col * j : gu_at + hidden_col * (j + 1)] for j in range(2)]
    )
    grad_a_down = col_sets[..., gu_at + 2 * hidden_col :]
    return (
        layer_out,
        input_grad,
        grad_a_qkv,
        grad_b_qkv,
        grad_a_out,
        grad_b_out,
        grad_a_gu,
        grad_b_gu,
        grad_a_down,
        grad_b_down,
    )


def solution(mesh):
    in_specs = (
        P(("dp", "col"), "row"),
        P(("dp", "col"), "row"),
        P("dp"),
        P("dp"),
        P("dp", None),
        P("dp"),
        P("col"),
        P("col"),
        P("row"),
        P("row"),
        P("row", None, "col"),
        P("col", "row"),
        P("row", None, "col"),
        P("col", "row"),
        P(None, None, None, "row"),
        P(None, None, None, "col"),
        P(None, None, "col"),
        P(None, None, "row"),
        P(None, None, None, "row"),
        P(None, None, None, "col"),
        P(None, None, "col"),
        P(None, None, "row"),
    )
    out_specs = (
        P(("dp", "col"), "row"),
        P(("dp", "col"), "row"),
        P(None, "dp", "col", "row"),
        P(None, "dp", "row", "col"),
        P("dp", "row", "col"),
        P("dp", "col", "row"),
        P(None, "dp", "col", "row"),
        P(None, "dp", "row", "col"),
        P("dp", "row", "col"),
        P("dp", "col", "row"),
    )
    return jax.shard_map(
        per_device, mesh=mesh, in_specs=in_specs, out_specs=out_specs, check_vma=False
    )
```

profile of v0, /device:TPU:0, one launch (start us, length us, event | category | flops | bytes accessed | tf_op | source)
XLA Modules:
  0.0 1157.8 jit_solution(14469267757178420043)
XLA Ops:
  7.2 14.6 %all_to_all.84 = bf16[4,160,512]{2,1,0:T(8,128)(2,1)S(1)} all-to-all(bf16[4,160,512]{2,1,0:T(8,128)(2,1)} %bitcast.270), channel_id=1, replica_groups=mesh['dp'=2,'row'=4,'col'=4] {'row'}, dimensions={0} | all-to-all | bytes 1310720 | tf_op jit(solution)/shard_map/all_to_all | solution.py:142
  28.9 6.3 all_gather.42
  39.2 39.6 %all-gather.11.cloned.1.call-done = bf16[640,2048]{1,0:T(8,128)(2,1)} async-done(((bf16[160,2048]{1,0:T(8,128)(2,1)}), bf16[640,2048]{1,0:T(8,128)(2,1)}) %all-gather.11.cloned.1.call-update) | async-done | bytes 2621456 | tf_op jit(solution)/shard_map/all_gather | solution.py:148
  84.6 40.9 %all-gather.13.cloned.1.call-done = bf16[2048,3,512]{0,2,1:T(8,128)(2,1)} async-done(((bf16[512,3,512]{0,2,1:T(8,128)(2,1)}), bf16[2048,3,512]{0,2,1:T(8,128)(2,1)}) %all-gather.13.cloned.1.call-update) | async-done | bytes 6291472 | tf_op jit(solution)/shard_map/all_gather | solution.py:134
  125.5 8.5 maximum_add_fusion
  137.0 12.3 %psum.14 = f32[2,640]{1,0:T(2,128)S(1)} all-reduce(f32[2,640]{1,0:T(2,128)S(1)} %pad_maximum_fusion.17), channel_id=1, replica_groups=mesh['dp'=2,'row'=4,'col'=4] {'col'}, use_global_device_ids=true, to_apply=%region_4.5 | all-reduce | flops 1280 | bytes 10240 | tf_op jit(solution)/shard_map/psum | solution.py:192
  169.0 4.8 copy.106
  173.8 4.6 all-to-all-start.1
  179.6 34.4 %all-to-all-done.1 = bf16[4,640,384]{1,2,0:T(8,128)(2,1)} async-done(((bf16[4,640,384]{1,2,0:T(8,128)(2,1)}), bf16[4,640,384]{1,2,0:T(8,128)(2,1)}, u32[]{:S(2)}, u32[]{:S(2)}) %all-to-all-start.1) | async-done | bytes 1966112 | tf_op jit(solution)/shard_map/all_to_all | solution.py:161
  219.8 8.5 fusion.114
  228.3 8.6 copy-done.2
  240.8 10.9 fusion.15
  251.8 12.7 %all_to_all.85 = bf16[4,640,128]{2,1,0:T(8,128)(2,1)S(1)} all-to-all(bf16[4,640,128]{2,1,0:T(8,128)(2,1)S(1)} %bitcast.254), channel_id=1, replica_groups=mesh['dp'=2,'row'=4,'col'=4] {'row'}, dimensions={0} | all-to-all | bytes 1310720 | tf_op jit(solution)/shard_map/all_to_all | solution.py:174
  272.8 5.2 all_gather.44
  278.0 43.6 %reduce-scatter.7.cloned.1.call-done = bf16[160,2048]{1,0:T(8,128)(2,1)} async-done(((bf16[640,2048]{1,0:T(8,128)(2,1)}), bf16[160,2048]{1,0:T(8,128)(2,1)}) %reduce-scatter.7.cloned.1.call-update) | async-done | bytes 655376 | tf_op jit(solution)/shard_map/reduce_scatter | solution.py:151
  327.8 52.1 %all-gather.17.cloned.1.call-done = bf16[640,2048]{1,0:T(8,128)(2,1)} async-done(((bf16[160,2048]{1,0:T(8,128)(2,1)}), bf16[640,2048]{1,0:T(8,128)(2,1)}) %all-gather.17.cloned.1.call-update) | async-done | bytes 2621456 | tf_op jit(solution)/shard_map/all_gather | solution.py:148
  382.5 103.5 %all-gather.19.cloned.1.call-done = bf16[2048,2,2048]{2,1,0:T(2,128)(2,1)} async-done(((bf16[512,2,2048]{2,1,0:T(2,128)(2,1)}), bf16[2048,2,2048]{2,1,0:T(2,128)(2,1)}) %all-gather.19.cloned.1.call-update) | async-done | bytes 16777232 | tf_op jit(solution)/shard_map/all_gather | solution.py:138
  486.0 13.0 %copy.133 = bf16[256,8,2,2048]{3,1,2,0:T(8,128)(2,1)S(1)} copy(bf16[256,8,2,2048]{3,2,1,0:T(2,128)(2,1)} %bitcast.231) | data formatting | bytes 33554432
  499.0 7.6 fusion.8
  509.9 7.3 fusion.4
  517.2 5.0 multiply_convert_fusion.3
  525.4 20.5 %all-gather.21.cloned.1.call-done = bf16[2048,2048]{1,0:T(8,128)(2,1)} async-done(((bf16[2048,512]{1,0:T(8,128)(2,1)}), bf16[2048,2048]{1,0:T(8,128)(2,1)}) %all-gather.21.cloned.1.call-update) | async-done | bytes 8388624 | tf_op jit(solution)/shard_map/all_gather | solution.py:139
  545.9 8.8 fusion.116
  559.0 12.6 %all_to_all.86 = bf16[4,160,512]{2,1,0:T(8,128)(2,1)S(1)} all-to-all(bf16[4,160,512]{2,1,0:T(8,128)(2,1)S(1)} %bitcast.271), channel_id=1, replica_groups=mesh['dp'=2,'row'=4,'col'=4] {'row'}, dimensions={0} | all-to-all | bytes 1310720 | tf_op jit(solution)/shard_map/all_to_all | solution.py:142
  571.9 38.2 %reduce-scatter.9.cloned.1.call-done = bf16[160,2048]{1,0:T(8,128)(2,1)} async-done(((bf16[640,2048]{1,0:T(8,128)(2,1)}), bf16[160,2048]{1,0:T(8,128)(2,1)}) %reduce-scatter.9.cloned.1.call-update) | async-done | bytes 655376 | tf_op jit(solution)/shard_map/reduce_scatter | solution.py:151
  614.8 54.1 %all-gather.23.cloned.1.call-done = bf16[640,2048]{1,0:T(8,128)(2,1)} async-done(((bf16[160,2048]{1,0:T(8,128)(2,1)}), bf16[640,2048]{1,0:T(8,128)(2,1)}) %all-gather.23.cloned.1.call-update) | async-done | bytes 2621456 | tf_op jit(solution)/shard_map/all_gather | solution.py:148
  668.9 11.2 fusion.117
  681.9 9.8 multiply_convert_fusion.1
  692.6 7.3 fusion.2
  702.6 7.5 fusion.6
  710.1 6.4 add_convert_fusion.1
  716.6 51.0 %reduce-scatter.11.cloned.1.call-done = bf16[160,2048]{1,0:T(8,128)(2,1)} async-done(((bf16[640,2048]{1,0:T(8,128)(2,1)}), bf16[160,2048]{1,0:T(8,128)(2,1)}) %reduce-scatter.11.cloned.1.call-update) | async-done | bytes 655376 | tf_op jit(solution)/shard_map/reduce_scatter | solution.py:151
  772.2 54.6 %all-gather.25.cloned.1.call-done = bf16[640,2048]{1,0:T(8,128)(2,1)} async-done(((bf16[160,2048]{1,0:T(8,128)(2,1)}), bf16[640,2048]{1,0:T(8,128)(2,1)}) %all-gather.25.cloned.1.call-update) | async-done | bytes 2621456 | tf_op jit(solution)/shard_map/all_gather | solution.py:148
  834.3 12.8 %all_to_all.87 = bf16[4,640,128]{2,1,0:T(8,128)(2,1)S(1)} all-to-all(bf16[4,640,128]{2,1,0:T(8,128)(2,1)S(1)} %bitcast.256), channel_id=1, replica_groups=mesh['dp'=2,'row'=4,'col'=4] {'row'}, dimensions={0} | all-to-all | bytes 1310720 | tf_op jit(solution)/shard_map/all_to_all | solution.py:161
  847.2 11.3 fusion.20
  858.5 20.5 %multiply_reduce_fusion = (f32[2560]{0:T(1024)S(1)}, f32[2560,2560]{0,1:T(8,128)}) fusion(f32[2560]{0:T(1024)S(1)} %copy-done.64, f32[2560,2560]{0,1:T(8,128)} %copy-done.2, f32[2560]{0:T(1024)S(1)} %copy-done.62, bf16[2560,128]{1,0:T(8,128)(2,1)S(1)} %bitcast.273, bf16[2560,384]{1,0:T(8,128)(2,1)S(1)} %bitcast.249), kind=kOutput, calls=%fused_computation.1 | convolution fusion | flops 1703933440 | bytes 53774336 | tf_op jit(solution)/shard_map/dot_general | solution.py:23
  878.9 22.4 %multiply_convert_fusion = bf16[2560,2560]{0,1:T(8,128)(2,1)} fusion(f32[2560,2560]{0,1:T(8,128)} %get-tuple-element.100, f32[2560]{0:T(1024)S(1)} %get-tuple-element.99, f32[2560]{0:T(1024)S(1)} %copy-done.64, f32[2560,2560]{0,1:T(8,128)} %copy-done.2, f32[2560]{0:T(1024)S(1)} %copy-done.62), kind=kLoop, calls=%fused_computation | loop fusion | flops 32768000 | bytes 65566720 | tf_op jit(solution)/shard_map/convert_element_type | solution.py:262
  901.3 9.1 fusion.18
  910.5 6.7 fusion.19
  933.0 17.8 %all-to-all-done.6 = bf16[4,640,384]{2,1,0:T(8,128)(2,1)S(1)} async-done(((bf16[4,640,384]{2,1,0:T(8,128)(2,1)}), bf16[4,640,384]{2,1,0:T(8,128)(2,1)S(1)}, u32[]{:S(2)}, u32[]{:S(2)}) %all-to-all-start.6) | async-done | bytes 1966112 | tf_op jit(solution)/shard_map/all_to_all | solution.py:174
  953.4 4.8 copy.118
  971.6 9.6 psum.15
  993.5 8.8 fusion.26
  1007.9 4.9 add_convert_fusion
  1028.9 12.6 %all-reduce.7.cloned.1.call-done = bf16[16,8192]{1,0:T(8,128)(2,1)} async-done(((bf16[16,8192]{1,0:T(8,128)(2,1)}), bf16[16,8192]{1,0:T(8,128)(2,1)}) %all-reduce.7.cloned.1.call-update) | async-done | bytes 262160
  1042.4 36.0 %all-reduce.5.cloned.1.call-done = bf16[4,7,4,512]{3,2,0,1:T(4,128)(2,1)} async-done(((bf16[4,7,4,512]{3,2,0,1:T(4,128)(2,1)}), bf16[4,7,4,512]{3,2,0,1:T(4,128)(2,1)}) %all-reduce.5.cloned.1.call-update) | async-done | bytes 114704
  1079.9 5.2 all-gather
  1091.2 41.5 %reduce-scatter.13.cloned.1.call-done = bf16[160,2048]{1,0:T(8,128)(2,1)} async-done(((bf16[640,2048]{1,0:T(8,128)(2,1)}), bf16[160,2048]{1,0:T(8,128)(2,1)}) %reduce-scatter.13.cloned.1.call-update) | async-done | bytes 655376 | tf_op jit(solution)/shard_map/reduce_scatter | solution.py:151
  (332 shorter events, 191.0 us)
Async XLA Ops:
  7.2 320.6 %copy-start = (f32[2,8,16,2048]{3,2,1,0:T(8,128)S(1)}, f32[2,8,16,2048]{3,2,1,0:T(8,128)}, u32[]{:S(2)}) copy-start(f32[2,8,16,2048]{3,2,1,0:T(8,128)} %param.41) | copy-start | bytes 6291460
  7.2 71.5 %all-gather.11.cloned.1.call-start = ((), (), s32[]{:S(2)}) async-start(), calls=%async_computation.13 | async-start | bytes 3276800 | tf_op jit(solution)/shard_map/all_gather | solution.py:148
  22.8 102.7 %all-gather.13.cloned.1.call-start = ((), (), s32[]{:S(2)}) async-start(), calls=%async_computation.14 | async-start | bytes 7864320 | tf_op jit(solution)/shard_map/all_gather | solution.py:134
  36.0 46.7 %copy-start.34 = (bf16[3,16,2048]{2,1,0:T(8,128)(2,1)}, bf16[3,16,2048]{2,1,0:T(8,128)(2,1)S(1)}, u32[]{:S(2)}) copy-start(bf16[3,16,2048]{2,1,0:T(8,128)(2,1)S(1)} %slice.228) | copy-start | bytes 589828
  37.0 47.2 %copy-start.43 = (bf16[3,1,16,512]{3,2,1,0:T(8,128)(2,1)}, bf16[3,1,16,512]{3,2,1,0:T(8,128)(2,1)S(1)}, u32[]{:S(2)}) copy-start(bf16[3,1,16,512]{3,2,1,0:T(8,128)(2,1)S(1)} %dynamic-slice_convert_fusion.2) | copy-start | bytes 147460
  134.0 15.4 %copy-start.65 = (f32[512]{0:T(512)S(1)}, f32[512]{0:T(512)}, u32[]{:S(2)}) copy-start(f32[512]{0:T(512)} %param.28) | copy-start | bytes 6148
  134.0 15.3 %copy-start.67 = (f32[512]{0:T(512)S(1)}, f32[512]{0:T(512)}, u32[]{:S(2)}) copy-start(f32[512]{0:T(512)} %param.29) | copy-start | bytes 6148
  173.8 40.1 %all-to-all-start.1 = ((bf16[4,640,384]{1,2,0:T(8,128)(2,1)}), bf16[4,640,384]{1,2,0:T(8,128)(2,1)}, u32[]{:S(2)}, u32[]{:S(2)}) async-start(bf16[4,640,384]{1,2,0:T(8,128)(2,1)} %bitcast.242), calls=%async_computation.1 | async-start | bytes 3932160 | tf_op jit(solution)/shard_map/all_to_all | solution.py:161
  178.4 87.4 %all-gather.15.cloned.1.call-start = ((), (), s32[]{:S(2)}) async-start(), calls=%async_computation.15 | async-start | bytes 2621440 | tf_op jit(solution)/shard_map/all_gather | solution.py:137
  179.1 142.5 %reduce-scatter.7.cloned.1.call-start = ((), (), s32[]{:S(2)}) async-start(), calls=%async_computation.16 | async-start | bytes 3276800 | tf_op jit(solution)/shard_map/reduce_scatter | solution.py:151
  219.8 21.0 %copy-start.28 = (bf16[4,4,160,384]{3,2,1,0:T(8,128)(2,1)}, bf16[4,4,160,384]{3,2,1,0:T(8,128)(2,1)S(1)}, u32[]{:S(2)}) copy-start(bf16[4,4,160,384]{3,2,1,0:T(8,128)(2,1)S(1)} %copy.108) | copy-start | bytes 5898244
  228.3 12.5 %copy-start.61 = (f32[2560]{0:T(1024)}, f32[2560]{0:T(1024)S(1)}, u32[]{:S(2)}) copy-start(f32[2560]{0:T(1024)S(1)} %get-tuple-element.95) | copy-start | bytes 30724
  240.8 10.9 copy-start.63
  272.1 50.8 %copy-start.20 = (bf16[4,20,8,512]{3,2,0,1:T(8,128)(2,1)S(1)}, bf16[4,20,8,512]{3,2,0,1:T(8,128)(2,1)}, u32[]{:S(2)}) copy-start(bf16[4,20,8,512]{3,2,0,1:T(8,128)(2,1)} %copy.129) | copy-start | bytes 1966084
  272.1 107.7 %all-gather.17.cloned.1.call-start = ((), (), s32[]{:S(2)}) async-start(), calls=%async_computation.17 | async-start | bytes 3276800 | tf_op jit(solution)/shard_map/all_gather | solution.py:148
  325.2 160.8 %all-gather.19.cloned.1.call-start = ((), (), s32[]{:S(2)}) async-start(), calls=%async_computation.18 | async-start | bytes 20971520 | tf_op jit(solution)/shard_map/all_gather | solution.py:138
  325.8 220.1 %all-gather.21.cloned.1.call-start = ((), (), s32[]{:S(2)}) async-start(), calls=%async_computation.19 | async-start | bytes 10485760 | tf_op jit(solution)/shard_map/all_gather | solution.py:139
  326.6 283.6 %reduce-scatter.9.cloned.1.call-start = ((), (), s32[]{:S(2)}) async-start(), calls=%async_computation.20 | async-start | bytes 3276800 | tf_op jit(solution)/shard_map/reduce_scatter | solution.py:151
  382.5 134.7 %copy-start.48 = (bf16[640,32]{0,1:T(8,128)(2,1)}, bf16[640,32]{0,1:T(8,128)(2,1)S(1)}, u32[]{:S(2)}) copy-start(bf16[640,32]{0,1:T(8,128)(2,1)S(1)} %convolution_convert_fusion.8) | copy-start | bytes 122884
  486.0 13.0 %copy-start.16 = (bf16[640,2048]{1,0:T(8,128)(2,1)S(1)}, bf16[640,2048]{1,0:T(8,128)(2,1)}, u32[]{:S(2)}) copy-start(bf16[640,2048]{1,0:T(8,128)(2,1)} %all-gather.17.cloned.1.call-done) | copy-start | bytes 7864324
  499.0 11.0 copy-start.7
  525.4 29.3 %copy-start.50 = (bf16[640,16]{0,1:T(8,128)(2,1)}, bf16[640,16]{0,1:T(8,128)(2,1)S(1)}, u32[]{:S(2)}) copy-start(bf16[640,16]{0,1:T(8,128)(2,1)S(1)} %convolution_convert_fusion.17) | copy-start | bytes 61444
  557.9 111.0 %all-gather.23.cloned.1.call-start = ((), (), s32[]{:S(2)}) async-start(), calls=%async_computation.21 | async-start | bytes 3276800 | tf_op jit(solution)/shard_map/all_gather | solution.py:148
  571.9 197.2 %copy-start.3 = (f32[4,20,8,512]{3,2,0,1:T(8,128)}, f32[4,20,8,512]{3,2,0,1:T(8,128)S(1)}, u32[]{:S(2)}) copy-start(f32[4,20,8,512]{3,2,0,1:T(8,128)S(1)} %copy.130) | copy-start | bytes 3932164
  614.3 153.3 %reduce-scatter.11.cloned.1.call-start = ((), (), s32[]{:S(2)}) async-start(), calls=%async_computation.22 | async-start | bytes 3276800 | tf_op jit(solution)/shard_map/reduce_scatter | solution.py:151
  668.9 11.2 copy-start.17
  680.1 12.4 %slice-start = ((s8[16777216]{0:T(1024)(128)(4,1)}), s8[4194304]{0:T(1024)(128)(4,1)S(1)}, s32[]{:S(2)}) async-start(s8[16777216]{0:T(1024)(128)(4,1)} %bitcast.227), calls=%async_computation.28 | async-start | bytes 8388608
  681.9 10.6 slice-start.1
  681.9 10.7 slice-start.2
  681.9 10.7 slice-start.3
  716.5 51.1 %copy-start.21 = (bf16[160,2048]{1,0:T(8,128)(2,1)S(1)}, bf16[160,2048]{1,0:T(8,128)(2,1)}, u32[]{:S(2)}) copy-start(bf16[160,2048]{1,0:T(8,128)(2,1)} %reduce-scatter.7.cloned.1.call-done) | copy-start | bytes 1966084
  716.5 110.3 %all-gather.25.cloned.1.call-start = ((), (), s32[]{:S(2)}) async-start(), calls=%async_computation.23 | async-start | bytes 3276800 | tf_op jit(solution)/shard_map/all_gather | solution.py:148
  832.8 14.4 %copy-start.62 = (f32[2560]{0:T(1024)S(1)}, f32[2560]{0:T(1024)}, u32[]{:S(2)}) copy-start(f32[2560]{0:T(1024)} %copy-done.61) | copy-start | bytes 30724
  832.8 14.4 %copy-start.64 = (f32[2560]{0:T(1024)S(1)}, f32[2560]{0:T(1024)}, u32[]{:S(2)}) copy-start(f32[2560]{0:T(1024)} %copy-done.63) | copy-start | bytes 30724
  847.2 11.3 copy-start.29
  922.8 28.0 %all-to-all-start.6 = ((bf16[4,640,384]{2,1,0:T(8,128)(2,1)}), bf16[4,640,384]{2,1,0:T(8,128)(2,1)S(1)}, u32[]{:S(2)}, u32[]{:S(2)}) async-start(bf16[4,640,384]{2,1,0:T(8,128)(2,1)} %bitcast.243), calls=%async_computation.9 | async-start | bytes 3932160 | tf_op jit(solution)/shard_map/all_to_all | solution.py:174
  926.6 79.7 %reduce-scatter.15.cloned.1.call-start = ((), (), s32[]{:S(2)}) async-start(), calls=%async_computation.25 | async-start | bytes 573440 | tf_op jit(solution)/shard_map/reduce_scatter | solution.py:284
  987.2 54.2 %all-reduce.7.cloned.1.call-start = ((), (), s32[]{:S(2)}) async-start(), calls=%async_computation.27 | async-start | bytes 524288
  993.5 84.9 %all-reduce.5.cloned.1.call-start = ((), (), s32[]{:S(2)}) async-start(), calls=%async_computation.26 | async-start | bytes 229376
  993.5 14.3 %copy-start.35 = (bf16[3,16,2048]{2,1,0:T(8,128)(2,1)S(1)}, bf16[3,16,2048]{2,1,0:T(8,128)(2,1)}, u32[]{:S(2)}) copy-start(bf16[3,16,2048]{2,1,0:T(8,128)(2,1)} %copy-done.34) | copy-start | bytes 589828
  1007.8 124.9 %reduce-scatter.13.cloned.1.call-start = ((), (), s32[]{:S(2)}) async-start(), calls=%async_computation.24 | async-start | bytes 3276800 | tf_op jit(solution)/shard_map/reduce_scatter | solution.py:151
  1014.8 14.1 %all-to-all-start.3 = ((bf16[160,4,512]{2,0,1:T(8,128)(2,1)}), bf16[160,4,512]{2,0,1:T(8,128)(2,1)S(1)}, u32[]{:S(2)}, u32[]{:S(2)}) async-start(bf16[160,4,512]{2,0,1:T(8,128)(2,1)} %bitcast.215), calls=%async_computation.5 | async-start | bytes 1310720 | tf_op jit(solution)/shard_map/all_to_all | solution.py:145
  1085.3 47.4 %copy-start.4 = (f32[4,20,8,512]{3,2,0,1:T(8,128)S(1)}, f32[4,20,8,512]{3,2,0,1:T(8,128)}, u32[]{:S(2)}) copy-start(f32[4,20,8,512]{3,2,0,1:T(8,128)} %copy-done.3) | copy-start | bytes 3932164
  1085.4 47.4 %copy-start.26 = (bf16[160,2048]{1,0:T(8,128)(2,1)S(1)}, bf16[160,2048]{1,0:T(8,128)(2,1)}, u32[]{:S(2)}) copy-start(bf16[160,2048]{1,0:T(8,128)(2,1)} %reduce-scatter.11.cloned.1.call-done) | copy-start | bytes 1966084
  1086.9 47.2 %copy-start.37 = (f32[4,7,4,512]{3,2,1,0:T(4,128)}, f32[4,7,4,512]{3,2,1,0:T(4,128)S(1)}, u32[]{:S(2)}) copy-start(f32[4,7,4,512]{3,2,1,0:T(4,128)S(1)} %reshape.348) | copy-start | bytes 688132
  1134.1 10.4 copy-start.42
  1135.0 15.9 %copy-start.1 = (f32[2,8,16,2048]{3,2,1,0:T(8,128)S(1)}, f32[2,8,16,2048]{3,2,1,0:T(8,128)}, u32[]{:S(2)}) copy-start(f32[2,8,16,2048]{3,2,1,0:T(8,128)} %param.41) | copy-start | bytes 6291460
  1135.0 13.8 %all-to-all-start.7 = ((bf16[160,4,512]{2,0,1:T(8,128)(2,1)}), bf16[160,4,512]{2,0,1:T(8,128)(2,1)S(1)}, u32[]{:S(2)}, u32[]{:S(2)}) async-start(bf16[160,4,512]{2,0,1:T(8,128)(2,1)} %bitcast.214), calls=%async_computation.11 | async-start | bytes 1310720 | tf_op jit(solution)/shard_map/all_to_all | solution.py:145
  (51 other events, 177.9 us)
Sparse Core Ops, SparseCore 0:
  22.9 55.7 all-gather.10
  80.3 45.1 all-gather.12
  180.8 32.5 all-gather.14
  272.3 49.3 reduce-scatter.6
  325.3 54.4 all-gather.16
  381.3 104.6 all-gather.18
  487.6 58.2 all-gather.20
  558.1 52.0 reduce-scatter.8
  614.4 54.4 all-gather.22
  716.7 50.8 reduce-scatter.10
  772.3 54.4 all-gather.24
  987.4 18.8 reduce-scatter.14
  1009.1 32.2 all-reduce.6
  1044.3 34.0 all-reduce.4
  1080.6 52.0 reduce-scatter.12
where the time goes:
time: 1170 us; the launch traced here: 1160 us
  waiting for transfers between devices  654 us (56%)
  matrix products  212 us (18%)
  local copies, waits for them, and re-layouts  96.2 us (8%)
  blocking collectives  95.6 us (8%)
  other arithmetic  66.5 us (6%)
  starting transfers between devices  16.8 us (1%)
  between operations  16.8 us (1%)
    all_gather x4, waiting for transfers between devices, gather_col(): return lax.all_gather(values, 'col', axis=0, tiled=True)  200 us
    reduce_scatter x4, waiting for transfers between devices, scatter_col(): lax.psum_scatter(values.astype(low), 'col', scatter_dimension=0, tiled=True)  174 us
    all_gather x1, waiting for transfers between devices, per_device(): lax.all_gather(gate_up_weight, 'row', axis=0, tiled=True)  104 us
    dot_general x18, matrix products, dot(): return jnp.dot(left, right, preferred_element_type=wide)  93.1 us
    dot_general x18, matrix products, dot_t(): return lax.dot_general(left, right, last_last, preferred_element_type=wide)  84.5 us
    unnamed x17, waiting for transfers between devices  50.7 us
    unnamed x173, local copies, waits for them, and re-layouts  41 us
    all_gather x1, waiting for transfers between devices, per_device(): lax.all_gather(query_key_value_weight, 'row', axis=0, tiled=True)  40.9 us
  transfers between devices with their start and end apart: 19, of which 18 were waited for; matrix products, arithmetic and copies ran while one was open for 11% of the time, Pallas kernels for 0%

commit v1 on v0

--- a/solution.py
+++ b/solution.py
@@ -13,6 +13,27 @@
 wide = jnp.float32
 last_last = (((1,), (1,)), ((), ()))
 first_first = (((0,), (0,)), ((), ()))
+
+
+def gather_around(x, axis, dim):
+    size, mine, rows = (lax.axis_size(axis), lax.axis_index(axis), x.shape[dim])
+    right = [(i, (i + 1) % size) for i in range(size)]
+    downward = [(i, (i - 1) % size) for i in range(size)]
+    whole = jnp.zeros((*x.shape[:dim], size * rows, *x.shape[dim + 1 :]), x.dtype)
+    whole = lax.dynamic_update_slice_in_dim(whole, x, mine * rows, axis=dim)
+    from_left = from_right = x
+    half = size // 2
+    for step in range(1, half + 1):
+        from_left = lax.ppermute(from_left, axis, right)
+        whole = lax.dynamic_update_slice_in_dim(
+            whole, from_left, (mine - step) % size * rows, axis=dim
+        )
+        if step < size - half:
+            from_right = lax.ppermute(from_right, axis, downward)
+            whole = lax.dynamic_update_slice_in_dim(
+                whole, from_right, (mine + step) % size * rows, axis=dim
+            )
+    return whole
 
 
 def dot(left, right):
@@ -145,7 +166,7 @@
         return lax.all_to_all(values, "row", split_axis=1, concat_axis=0, tiled=True)
 
     def gather_col(values):
-        return lax.all_gather(values, "col", axis=0, tiled=True)
+        return gather_around(values, "col", 0)
 
     def scatter_col(values):
         return lax.psum_scatter(values.astype(low), "col", scatter_dimension=0, tiled=True).astype(

time: 1170 us -> 1030 us (0.88)
  waiting for transfers between devices: 654 us -> 483 us
  starting transfers between devices: 16.8 us -> 71.7 us
  blocking collectives: 95.6 us -> 81.7 us
    all_gather x4 -> x0, waiting for transfers between devices: 200 us -> none  [gather_col(): return lax.all_gather(values, 'col', axis=0, tiled=True)]
    ppermute x0 -> x12, waiting for transfers between devices: none -> 119 us  [the longest x8 105 us: gather_around(): from_left = lax.ppermute(from_left, axis, right)]
    all_gather x1, waiting for transfers between devices: 104 us -> 51.2 us  [per_device(): lax.all_gather(gate_up_weight, 'row', axis=0, tiled=True)]
    ppermute x0 -> x12, starting transfers between devices: none -> 51 us  [the longest x8 39.3 us: gather_around(): from_left = lax.ppermute(from_left, axis, right)]
    all_gather x1, waiting for transfers between devices: 40.9 us -> 0.01 us  [per_device(): lax.all_gather(query_key_value_weight, 'row', axis=0, tiled=True)]
    all_to_all x2 -> x1, blocking collectives: 27.3 us -> 12.6 us  [to_tokens(): lax.all_to_all(values, 'row', split_axis=0, concat_axis=1, tiled=True)]
    unnamed x17 -> x13, waiting for transfers between devices: 50.7 us -> 50.3 us
    unnamed x173 -> x189, local copies, waits for them, and re-layouts: 41 us -> 40.6 us
  transfers between devices with their start and end apart: 19 -> 28, of which waited for: 18 -> 26; matrix products, arithmetic and copies ran while one was open for 11% -> 14% of each run, Pallas kernels for 0% -> 0%
where the time goes in v1:
time: 1030 us; the launch traced here: 1020 us
  waiting for transfers between devices  483 us (47%)
  matrix products  206 us (20%)
  local copies, waits for them, and re-layouts  99.7 us (10%)
  blocking collectives  81.7 us (8%)
  starting transfers between devices  71.7 us (7%)
  other arithmetic  62.6 us (6%)
  between operations  17 us (2%)
    reduce_scatter x4, waiting for transfers between devices, scatter_col(): lax.psum_scatter(values.astype(low), 'col', scatter_dimension=0, tiled=True)  172 us
    ppermute x8, waiting for transfers between devices, gather_around(): from_left = lax.ppermute(from_left, axis, right)  105 us
    dot_general x18, matrix products, dot(): return jnp.dot(left, right, preferred_element_type=wide)  87 us
    dot_general x18, matrix products, dot_t(): return lax.dot_general(left, right, last_last, preferred_element_type=wide)  83.4 us
    all_gather x1, waiting for transfers between devices, per_device(): lax.all_gather(gate_up_weight, 'row', axis=0, tiled=True)  51.2 us
    unnamed x13, waiting for transfers between devices  50.3 us
    unnamed x189, local copies, waits for them, and re-layouts  40.6 us
    ppermute x8, starting transfers between devices, gather_around(): from_left = lax.ppermute(from_left, axis, right)  39.3 us
  transfers between devices with their start and end apart: 28, of which 26 were waited for; matrix products, arithmetic and copies ran while one was open for 14% of the time, Pallas kernels for 0%

profile of v1, /device:TPU:0, one launch (start us, length us, event | category | flops | bytes accessed | tf_op | source)
XLA Modules:
  0.0 1021.7 jit_solution(699693094470632886)
XLA Ops:
  17.4 8.2 all-to-all-done
  33.3 9.2 all_gather.29
  48.2 12.4 %collective-permute-done.1 = bf16[160,2048]{1,0:T(8,128)(2,1)} collective-permute-done((bf16[160,2048]{1,0:T(8,128)(2,1)S(1)}, bf16[160,2048]{1,0:T(8,128)(2,1)}, u32[]{:S(2)}, u32[]{:S(2)}) %collective-permute-start.1) | collective-permute-done | bytes 655392 | tf_op jit(solution)/shard_map/ppermute | solution.py:32
  61.7 10.9 %collective-permute-done.2 = bf16[160,2048]{1,0:T(8,128)(2,1)S(1)} collective-permute-done((bf16[160,2048]{1,0:T(8,128)(2,1)}, bf16[160,2048]{1,0:T(8,128)(2,1)S(1)}, u32[]{:S(2)}, u32[]{:S(2)}) %collective-permute-start.2) | collective-permute-done | bytes 655392 | tf_op jit(solution)/shard_map/ppermute | solution.py:27
  77.1 8.5 maximum_add_fusion
  88.6 10.4 %psum.14 = f32[2,640]{1,0:T(2,128)S(1)} all-reduce(f32[2,640]{1,0:T(2,128)S(1)} %pad_maximum_fusion.17), channel_id=1, replica_groups=mesh['dp'=2,'row'=4,'col'=4] {'col'}, use_global_device_ids=true, to_apply=%region_4.5 | all-reduce | flops 1280 | bytes 10240 | tf_op jit(solution)/shard_map/psum | solution.py:213
  129.0 34.3 %all-to-all-done.1 = bf16[4,640,384]{1,2,0:T(8,128)(2,1)} async-done(((bf16[4,640,384]{1,2,0:T(8,128)(2,1)}), bf16[4,640,384]{1,2,0:T(8,128)(2,1)}, u32[]{:S(2)}, u32[]{:S(2)}) %all-to-all-start.1) | async-done | bytes 1966112 | tf_op jit(solution)/shard_map/all_to_all | solution.py:182
  169.1 8.5 fusion.126
  177.7 8.6 copy-done.2
  190.2 10.9 %fusion.15 = bf16[2560,128]{1,0:T(8,128)(2,1)S(1)} fusion(bf16[2560,384]{1,0:T(8,128)(2,1)S(1)} %bitcast.242, f32[2560,2560]{0,1:T(8,128)} %copy-done.2, f32[2560]{0:T(1024)S(1)} %fusion.1, f32[2560]{0:T(1024)S(1)} %get-tuple-element.101), kind=kOutput, calls=%fused_computation.30 | convolution fusion | flops 1697710080 | bytes 27549696 | tf_op jit(solution)/shard_map/dot_general | solution.py:40
  201.1 12.7 %all_to_all.84 = bf16[4,640,128]{2,1,0:T(8,128)(2,1)S(1)} all-to-all(bf16[4,640,128]{2,1,0:T(8,128)(2,1)S(1)} %bitcast.249), channel_id=1, replica_groups=mesh['dp'=2,'row'=4,'col'=4] {'row'}, dimensions={0} | all-to-all | bytes 1310720 | tf_op jit(solution)/shard_map/all_to_all | solution.py:195
  222.0 5.2 all_gather.31
  227.2 43.1 %reduce-scatter.7.cloned.1.call-done = bf16[160,2048]{1,0:T(8,128)(2,1)} async-done(((bf16[640,2048]{1,0:T(8,128)(2,1)}), bf16[160,2048]{1,0:T(8,128)(2,1)}) %reduce-scatter.7.cloned.1.call-update) | async-done | bytes 655376 | tf_op jit(solution)/shard_map/reduce_scatter | solution.py:172
  276.2 15.6 %collective-permute-done.3 = bf16[160,2048]{1,0:T(8,128)(2,1)S(1)} collective-permute-done((bf16[160,2048]{1,0:T(8,128)(2,1)S(1)}, bf16[160,2048]{1,0:T(8,128)(2,1)S(1)}, u32[]{:S(2)}, u32[]{:S(2)}) %collective-permute-start.3) | collective-permute-done | bytes 655392 | tf_op jit(solution)/shard_map/ppermute | solution.py:27
  291.9 11.6 %collective-permute-start.5 = (bf16[160,2048]{1,0:T(8,128)(2,1)S(1)}, bf16[160,2048]{1,0:T(8,128)(2,1)S(1)}, u32[]{:S(2)}, u32[]{:S(2)}) collective-permute-start(bf16[160,2048]{1,0:T(8,128)(2,1)S(1)} %collective-permute-done.3), channel_id=1, source_target_pairs={{0,1},{1,2},{2,3},{3,0},{4,5},{5,6},{6,7},{7,4},{8,9},{9,10},{10,1... | collective-permute-start | bytes 1966088 | tf_op jit(solution)/shard_map/ppermute | solution.py:27
  304.0 14.6 %collective-permute-done.5 = bf16[160,2048]{1,0:T(8,128)(2,1)S(1)} collective-permute-done((bf16[160,2048]{1,0:T(8,128)(2,1)S(1)}, bf16[160,2048]{1,0:T(8,128)(2,1)S(1)}, u32[]{:S(2)}, u32[]{:S(2)}) %collective-permute-start.5) | collective-permute-done | bytes 655392 | tf_op jit(solution)/shard_map/ppermute | solution.py:27
  326.1 51.2 %all-gather.11.cloned.1.call-done = bf16[2048,2,2048]{2,1,0:T(2,128)(2,1)} async-done(((bf16[512,2,2048]{2,1,0:T(2,128)(2,1)}), bf16[2048,2,2048]{2,1,0:T(2,128)(2,1)}) %all-gather.11.cloned.1.call-update) | async-done | bytes 16777232 | tf_op jit(solution)/shard_map/all_gather | solution.py:159
  377.3 13.0 %copy.133 = bf16[256,8,2,2048]{3,1,2,0:T(8,128)(2,1)S(1)} copy(bf16[256,8,2,2048]{3,2,1,0:T(2,128)(2,1)} %bitcast.223) | data formatting | bytes 33554432
  390.3 11.3 %fusion.23 = f32[640,2048]{1,0:T(8,128)} fusion(f32[640,2048]{1,0:T(8,128)} %fusion.74, bf16[640,2048]{1,0:T(8,128)(2,1)S(1)} %copy-done.13, bf16[2048,4096]{1,0:T(8,128)(2,1)S(1)} %bitcast.219), kind=kOutput, calls=%fused_computation.35 | convolution fusion | flops 5370019840 | bytes 21495808 | tf_op jit(solution)/shard_map/dot_general | solution.py:40
  401.6 11.0 %multiply_convert_fusion.3 = (bf16[640,2048]{1,0:T(8,128)(2,1)}, f32[640,2048]{1,0:T(8,128)}) fusion(f32[640,2048]{1,0:T(8,128)} %fusion.23, f32[640,2048]{1,0:T(8,128)} %fusion.75, bf16[640,2048]{1,0:T(8,128)(2,1)S(1)} %copy-done.13, bf16[2048,4096]{1,0:T(8,128)(2,1)S(1)} %bitcast.220), kind=kOutput, calls=%fused_computation.23 | convolution fusion | flops 5377884160 | bytes 29360128 | tf_op jit(solution)/shard_map/dot_general | solution.py:40
  415.1 21.9 %all-gather.13.cloned.1.call-done = bf16[2048,2048]{1,0:T(8,128)(2,1)} async-done(((bf16[2048,512]{1,0:T(8,128)(2,1)}), bf16[2048,2048]{1,0:T(8,128)(2,1)}) %all-gather.13.cloned.1.call-update) | async-done | bytes 8388624 | tf_op jit(solution)/shard_map/all_gather | solution.py:160
  437.0 8.8 fusion.128
  449.3 12.6 %all_to_all.85 = bf16[4,160,512]{2,1,0:T(8,128)(2,1)S(1)} all-to-all(bf16[4,160,512]{2,1,0:T(8,128)(2,1)S(1)} %bitcast.263), channel_id=1, replica_groups=mesh['dp'=2,'row'=4,'col'=4] {'row'}, dimensions={0} | all-to-all | bytes 1310720 | tf_op jit(solution)/shard_map/all_to_all | solution.py:163
  462.2 38.2 %reduce-scatter.9.cloned.1.call-done = bf16[160,2048]{1,0:T(8,128)(2,1)} async-done(((bf16[640,2048]{1,0:T(8,128)(2,1)}), bf16[160,2048]{1,0:T(8,128)(2,1)}) %reduce-scatter.9.cloned.1.call-update) | async-done | bytes 655376 | tf_op jit(solution)/shard_map/reduce_scatter | solution.py:172
  507.9 15.7 %collective-permute-done.6 = bf16[160,2048]{1,0:T(8,128)(2,1)S(1)} collective-permute-done((bf16[160,2048]{1,0:T(8,128)(2,1)S(1)}, bf16[160,2048]{1,0:T(8,128)(2,1)S(1)}, u32[]{:S(2)}, u32[]{:S(2)}) %collective-permute-start.6) | collective-permute-done | bytes 655392 | tf_op jit(solution)/shard_map/ppermute | solution.py:27
  523.5 11.2 %collective-permute-start.8 = (bf16[160,2048]{1,0:T(8,128)(2,1)S(1)}, bf16[160,2048]{1,0:T(8,128)(2,1)S(1)}, u32[]{:S(2)}, u32[]{:S(2)}) collective-permute-start(bf16[160,2048]{1,0:T(8,128)(2,1)S(1)} %collective-permute-done.6), channel_id=1, source_target_pairs={{0,1},{1,2},{2,3},{3,0},{4,5},{5,6},{6,7},{7,4},{8,9},{9,10},{10,1... | collective-permute-start | bytes 1966088 | tf_op jit(solution)/shard_map/ppermute | solution.py:27
  535.7 14.6 %collective-permute-done.8 = bf16[160,2048]{1,0:T(8,128)(2,1)S(1)} collective-permute-done((bf16[160,2048]{1,0:T(8,128)(2,1)S(1)}, bf16[160,2048]{1,0:T(8,128)(2,1)S(1)}, u32[]{:S(2)}, u32[]{:S(2)}) %collective-permute-start.8) | collective-permute-done | bytes 655392 | tf_op jit(solution)/shard_map/ppermute | solution.py:27
  556.1 15.9 %multiply_convert_fusion.1 = (bf16[640,2048]{1,0:T(8,128)(2,1)}, bf16[640,2048]{1,0:T(8,128)(2,1)}) fusion(f32[640,2048]{1,0:T(8,128)} %fusion.23, f32[640,2048]{1,0:T(8,128)} %get-tuple-element.104, f32[640,2048]{1,0:T(8,128)} %fusion.78, bf16[640,2048]{1,0:T(8,128)(2,1)S(1)} %constant_dynamic-update-slice_fusion.4, ...), kind=kOutput, calls=%fused_computation.20 | convolution fusion | flops 5387059200 | bytes 31981568 | tf_op jit(solution)/shard_map/dot_general | solution.py:44
  572.0 9.0 fusion.2
  582.8 8.0 fusion.6
  594.6 50.6 %reduce-scatter.11.cloned.1.call-done = bf16[160,2048]{1,0:T(8,128)(2,1)} async-done(((bf16[640,2048]{1,0:T(8,128)(2,1)}), bf16[160,2048]{1,0:T(8,128)(2,1)}) %reduce-scatter.11.cloned.1.call-update) | async-done | bytes 655376 | tf_op jit(solution)/shard_map/reduce_scatter | solution.py:172
  652.7 15.7 %collective-permute-done.9 = bf16[160,2048]{1,0:T(8,128)(2,1)S(1)} collective-permute-done((bf16[160,2048]{1,0:T(8,128)(2,1)S(1)}, bf16[160,2048]{1,0:T(8,128)(2,1)S(1)}, u32[]{:S(2)}, u32[]{:S(2)}) %collective-permute-start.9) | collective-permute-done | bytes 655392 | tf_op jit(solution)/shard_map/ppermute | solution.py:27
  668.3 11.5 %collective-permute-start.11 = (bf16[160,2048]{1,0:T(8,128)(2,1)S(1)}, bf16[160,2048]{1,0:T(8,128)(2,1)S(1)}, u32[]{:S(2)}, u32[]{:S(2)}) collective-permute-start(bf16[160,2048]{1,0:T(8,128)(2,1)S(1)} %collective-permute-done.9), channel_id=1, source_target_pairs={{0,1},{1,2},{2,3},{3,0},{4,5},{5,6},{6,7},{7,4},{8,9},{9,10},{10,1... | collective-permute-start | bytes 1966088 | tf_op jit(solution)/shard_map/ppermute | solution.py:27
  680.5 14.6 %collective-permute-done.11 = bf16[160,2048]{1,0:T(8,128)(2,1)S(1)} collective-permute-done((bf16[160,2048]{1,0:T(8,128)(2,1)S(1)}, bf16[160,2048]{1,0:T(8,128)(2,1)S(1)}, u32[]{:S(2)}, u32[]{:S(2)}) %collective-permute-start.11) | collective-permute-done | bytes 655392 | tf_op jit(solution)/shard_map/ppermute | solution.py:27
  700.8 12.9 %all_to_all.86 = bf16[4,640,128]{2,1,0:T(8,128)(2,1)S(1)} all-to-all(bf16[4,640,128]{2,1,0:T(8,128)(2,1)S(1)} %bitcast.251), channel_id=1, replica_groups=mesh['dp'=2,'row'=4,'col'=4] {'row'}, dimensions={0} | all-to-all | bytes 1310720 | tf_op jit(solution)/shard_map/all_to_all | solution.py:182
  713.8 20.4 %multiply_reduce_fusion = (f32[2560]{0:T(1024)S(1)}, f32[2560,2560]{0,1:T(8,128)}) fusion(f32[2560]{0:T(1024)S(1)} %copy-done.76, f32[2560,2560]{0,1:T(8,128)} %copy-done.2, f32[2560]{0:T(1024)S(1)} %copy-done.74, bf16[2560,128]{1,0:T(8,128)(2,1)S(1)} %bitcast.264, bf16[2560,384]{1,0:T(8,128)(2,1)S(1)} %bitcast.243), kind=kOutput, calls=%fused_computation.1 | convolution fusion | flops 1703933440 | bytes 53774336 | tf_op jit(solution)/shard_map/dot_general | solution.py:44
  734.2 22.4 %multiply_convert_fusion = bf16[2560,2560]{0,1:T(8,128)(2,1)} fusion(f32[2560,2560]{0,1:T(8,128)} %get-tuple-element.106, f32[2560]{0:T(1024)S(1)} %get-tuple-element.105, f32[2560]{0:T(1024)S(1)} %copy-done.76, f32[2560,2560]{0,1:T(8,128)} %copy-done.2, f32[2560]{0:T(1024)S(1)} %copy-done.74), kind=kLoop, calls=%fused_computation | loop fusion | flops 32768000 | bytes 65566720 | tf_op jit(solution)/shard_map/convert_element_type | solution.py:283
  756.6 6.7 fusion.19
  763.2 9.1 fusion.18
  772.4 11.1 %fusion.20 = bf16[2560,128]{0,1:T(8,128)(2,1)S(1)} fusion(bf16[2560,128]{1,0:T(8,128)(2,1)S(1)} %bitcast.265, f32[2560,2560]{0,1:T(8,128)} %copy-done.2, f32[2560]{0:T(1024)S(1)} %copy-done.76, f32[2560]{0:T(1024)S(1)} %copy-done.74), kind=kOutput, calls=%fused_computation.33 | convolution fusion | flops 1697710080 | bytes 27545600 | tf_op jit(solution)/shard_map/dot_general | solution.py:48
  799.6 17.6 %all-to-all-done.6 = bf16[4,640,384]{2,1,0:T(8,128)(2,1)S(1)} async-done(((bf16[4,640,384]{2,1,0:T(8,128)(2,1)}), bf16[4,640,384]{2,1,0:T(8,128)(2,1)S(1)}, u32[]{:S(2)}, u32[]{:S(2)}) %all-to-all-start.6) | async-done | bytes 1966112 | tf_op jit(solution)/shard_map/all_to_all | solution.py:195
  837.1 9.3 psum.15
  859.9 8.8 fusion.32
  871.9 4.8 add_convert_fusion
  893.0 12.4 %all-reduce.7.cloned.1.call-done = bf16[16,8192]{1,0:T(8,128)(2,1)} async-done(((bf16[16,8192]{1,0:T(8,128)(2,1)}), bf16[16,8192]{1,0:T(8,128)(2,1)}) %all-reduce.7.cloned.1.call-update) | async-done | bytes 262160
  906.4 36.0 %all-reduce.5.cloned.1.call-done = bf16[4,7,4,512]{3,2,0,1:T(4,128)(2,1)} async-done(((bf16[4,7,4,512]{3,2,0,1:T(4,128)(2,1)}), bf16[4,7,4,512]{3,2,0,1:T(4,128)(2,1)}) %all-reduce.5.cloned.1.call-update) | async-done | bytes 114704
  943.8 5.2 all-gather
  956.7 40.1 %reduce-scatter.13.cloned.1.call-done = bf16[160,2048]{1,0:T(8,128)(2,1)} async-done(((bf16[640,2048]{1,0:T(8,128)(2,1)}), bf16[160,2048]{1,0:T(8,128)(2,1)}) %reduce-scatter.13.cloned.1.call-update) | async-done | bytes 655376 | tf_op jit(solution)/shard_map/reduce_scatter | solution.py:172
  (377 shorter events, 228.3 us)
Async XLA Ops:
  7.2 296.3 %copy-start = (f32[2,8,16,2048]{3,2,1,0:T(8,128)S(1)}, f32[2,8,16,2048]{3,2,1,0:T(8,128)}, u32[]{:S(2)}) copy-start(f32[2,8,16,2048]{3,2,1,0:T(8,128)} %param.41) | copy-start | bytes 6291460
  7.2 69.9 %all-gather.7.cloned.1.call-start = ((), (), s32[]{:S(2)}) async-start(), calls=%async_computation.13 | async-start | bytes 7864320 | tf_op jit(solution)/shard_map/all_gather | solution.py:155
  10.0 18.7 %copy-start.81 = (s32[2560]{0:T(1024)S(1)}, s32[2560]{0:T(1024)}, u32[]{:S(2)}) copy-start(s32[2560]{0:T(1024)} %param.25) | copy-start | bytes 30724
  10.0 15.7 %all-to-all-start = ((bf16[4,160,512]{2,1,0:T(8,128)(2,1)}), bf16[4,160,512]{2,1,0:T(8,128)(2,1)S(1)}, u32[]{:S(2)}, u32[]{:S(2)}) async-start(bf16[4,160,512]{2,1,0:T(8,128)(2,1)} %bitcast), calls=%async_computation | async-start | bytes 1310720 | tf_op jit(solution)/shard_map/all_to_all | solution.py:163
  25.8 21.3 %copy-start.21 = (bf16[4,20,8,512]{3,2,0,1:T(8,128)(2,1)}, bf16[4,20,8,512]{3,2,0,1:T(8,128)(2,1)S(1)}, u32[]{:S(2)}) copy-start(bf16[4,20,8,512]{3,2,0,1:T(8,128)(2,1)S(1)} %copy.129) | copy-start | bytes 1966084
  25.8 20.9 %collective-permute-start = (bf16[160,2048]{1,0:T(8,128)(2,1)S(1)}, bf16[160,2048]{1,0:T(8,128)(2,1)}, u32[]{:S(2)}, u32[]{:S(2)}) collective-permute-start(bf16[160,2048]{1,0:T(8,128)(2,1)S(1)} %bitcast.231), channel_id=1, source_target_pairs={{0,1},{1,2},{2,3},{3,0},{4,5},{5,6},{6,7},{7,4},{8,9},{9,10},{10,1... | collective-permute-start | bytes 1966088 | tf_op jit(solution)/shard_map/ppermute | solution.py:27
  31.1 29.5 %collective-permute-start.1 = (bf16[160,2048]{1,0:T(8,128)(2,1)S(1)}, bf16[160,2048]{1,0:T(8,128)(2,1)}, u32[]{:S(2)}, u32[]{:S(2)}) collective-permute-start(bf16[160,2048]{1,0:T(8,128)(2,1)S(1)} %bitcast.232), channel_id=1, source_target_pairs={{0,3},{1,0},{2,1},{3,2},{4,7},{5,4},{6,5},{7,6},{8,11},{9,8},{10,9... | collective-permute-start | bytes 1966088 | tf_op jit(solution)/shard_map/ppermute | solution.py:32
  42.5 30.3 %copy-start.40 = (bf16[3,16,2048]{2,1,0:T(8,128)(2,1)}, bf16[3,16,2048]{2,1,0:T(8,128)(2,1)S(1)}, u32[]{:S(2)}) copy-start(bf16[3,16,2048]{2,1,0:T(8,128)(2,1)S(1)} %slice.228) | copy-start | bytes 589828
  43.5 32.2 %copy-start.50 = (bf16[3,1,16,512]{3,2,1,0:T(8,128)(2,1)}, bf16[3,1,16,512]{3,2,1,0:T(8,128)(2,1)S(1)}, u32[]{:S(2)}) copy-start(bf16[3,1,16,512]{3,2,1,0:T(8,128)(2,1)S(1)} %dynamic-slice_convert_fusion.2) | copy-start | bytes 147460
  46.6 26.0 %collective-permute-start.2 = (bf16[160,2048]{1,0:T(8,128)(2,1)}, bf16[160,2048]{1,0:T(8,128)(2,1)S(1)}, u32[]{:S(2)}, u32[]{:S(2)}) collective-permute-start(bf16[160,2048]{1,0:T(8,128)(2,1)} %collective-permute-done), channel_id=1, source_target_pairs={{0,1},{1,2},{2,3},{3,0},{4,5},{5,6},{6,7},{7,4},{8,9},{9,10},{10,1... | collective-permute-start | bytes 1966088 | tf_op jit(solution)/shard_map/ppermute | solution.py:27
  85.7 13.4 %copy-start.77 = (f32[512]{0:T(512)S(1)}, f32[512]{0:T(512)}, u32[]{:S(2)}) copy-start(f32[512]{0:T(512)} %param.28) | copy-start | bytes 6148
  85.7 13.4 %copy-start.79 = (f32[512]{0:T(512)S(1)}, f32[512]{0:T(512)}, u32[]{:S(2)}) copy-start(f32[512]{0:T(512)} %param.29) | copy-start | bytes 6148
  123.2 40.2 %all-to-all-start.1 = ((bf16[4,640,384]{1,2,0:T(8,128)(2,1)}), bf16[4,640,384]{1,2,0:T(8,128)(2,1)}, u32[]{:S(2)}, u32[]{:S(2)}) async-start(bf16[4,640,384]{1,2,0:T(8,128)(2,1)} %bitcast.236), calls=%async_computation.1 | async-start | bytes 3932160 | tf_op jit(solution)/shard_map/all_to_all | solution.py:182
  127.7 87.3 %all-gather.9.cloned.1.call-start = ((), (), s32[]{:S(2)}) async-start(), calls=%async_computation.14 | async-start | bytes 2621440 | tf_op jit(solution)/shard_map/all_gather | solution.py:158
  128.5 141.8 %reduce-scatter.7.cloned.1.call-start = ((), (), s32[]{:S(2)}) async-start(), calls=%async_computation.15 | async-start | bytes 3276800 | tf_op jit(solution)/shard_map/reduce_scatter | solution.py:172
  169.1 21.0 %copy-start.32 = (bf16[4,4,160,384]{3,2,1,0:T(8,128)(2,1)}, bf16[4,4,160,384]{3,2,1,0:T(8,128)(2,1)S(1)}, u32[]{:S(2)}) copy-start(bf16[4,4,160,384]{3,2,1,0:T(8,128)(2,1)S(1)} %copy.108) | copy-start | bytes 5898244
  220.7 156.6 %all-gather.11.cloned.1.call-start = ((), (), s32[]{:S(2)}) async-start(), calls=%async_computation.16 | async-start | bytes 20971520 | tf_op jit(solution)/shard_map/all_gather | solution.py:159
  221.3 50.7 %copy-start.22 = (bf16[4,20,8,512]{3,2,0,1:T(8,128)(2,1)S(1)}, bf16[4,20,8,512]{3,2,0,1:T(8,128)(2,1)}, u32[]{:S(2)}) copy-start(bf16[4,20,8,512]{3,2,0,1:T(8,128)(2,1)} %copy-done.21) | copy-start | bytes 1966084
  221.3 215.7 %all-gather.13.cloned.1.call-start = ((), (), s32[]{:S(2)}) async-start(), calls=%async_computation.17 | async-start | bytes 10485760 | tf_op jit(solution)/shard_map/all_gather | solution.py:160
  221.9 278.6 %reduce-scatter.9.cloned.1.call-start = ((), (), s32[]{:S(2)}) async-start(), calls=%async_computation.18 | async-start | bytes 3276800 | tf_op jit(solution)/shard_map/reduce_scatter | solution.py:172
  272.4 19.5 %collective-permute-start.3 = (bf16[160,2048]{1,0:T(8,128)(2,1)S(1)}, bf16[160,2048]{1,0:T(8,128)(2,1)S(1)}, u32[]{:S(2)}, u32[]{:S(2)}) collective-permute-start(bf16[160,2048]{1,0:T(8,128)(2,1)S(1)} %get-tuple-element.63), channel_id=1, source_target_pairs={{0,1},{1,2},{2,3},{3,0},{4,5},{5,6},{6,7},{7,4},{8,9},{9,10},{10,1... | collective-permute-start | bytes 1966088 | tf_op jit(solution)/shard_map/ppermute | solution.py:27
  273.1 30.9 %collective-permute-start.4 = (bf16[160,2048]{1,0:T(8,128)(2,1)S(1)}, bf16[160,2048]{1,0:T(8,128)(2,1)S(1)}, u32[]{:S(2)}, u32[]{:S(2)}) collective-permute-start(bf16[160,2048]{1,0:T(8,128)(2,1)S(1)} %get-tuple-element.63), channel_id=1, source_target_pairs={{0,3},{1,0},{2,1},{3,2},{4,7},{5,4},{6,5},{7,6},{8,11},{9,8},{10,9... | collective-permute-start | bytes 1966088 | tf_op jit(solution)/shard_map/ppermute | solution.py:32
  291.9 26.7 %collective-permute-start.5 = (bf16[160,2048]{1,0:T(8,128)(2,1)S(1)}, bf16[160,2048]{1,0:T(8,128)(2,1)S(1)}, u32[]{:S(2)}, u32[]{:S(2)}) collective-permute-start(bf16[160,2048]{1,0:T(8,128)(2,1)S(1)} %collective-permute-done.3), channel_id=1, source_target_pairs={{0,1},{1,2},{2,3},{3,0},{4,5},{5,6},{6,7},{7,4},{8,9},{9,10},{10,1... | collective-permute-start | bytes 1966088 | tf_op jit(solution)/shard_map/ppermute | solution.py:27
  415.1 30.7 %copy-start.55 = (bf16[640,16]{0,1:T(8,128)(2,1)}, bf16[640,16]{0,1:T(8,128)(2,1)S(1)}, u32[]{:S(2)}) copy-start(bf16[640,16]{0,1:T(8,128)(2,1)S(1)} %convolution_convert_fusion.17) | copy-start | bytes 61444
  448.2 197.0 %reduce-scatter.11.cloned.1.call-start = ((), (), s32[]{:S(2)}) async-start(), calls=%async_computation.19 | async-start | bytes 3276800 | tf_op jit(solution)/shard_map/reduce_scatter | solution.py:172
  462.2 186.1 %copy-start.3 = (f32[4,20,8,512]{3,2,0,1:T(8,128)}, f32[4,20,8,512]{3,2,0,1:T(8,128)S(1)}, u32[]{:S(2)}) copy-start(f32[4,20,8,512]{3,2,0,1:T(8,128)S(1)} %copy.130) | copy-start | bytes 3932164
  504.0 19.5 %collective-permute-start.6 = (bf16[160,2048]{1,0:T(8,128)(2,1)S(1)}, bf16[160,2048]{1,0:T(8,128)(2,1)S(1)}, u32[]{:S(2)}, u32[]{:S(2)}) collective-permute-start(bf16[160,2048]{1,0:T(8,128)(2,1)S(1)} %get-tuple-element.61), channel_id=1, source_target_pairs={{0,1},{1,2},{2,3},{3,0},{4,5},{5,6},{6,7},{7,4},{8,9},{9,10},{10,1... | collective-permute-start | bytes 1966088 | tf_op jit(solution)/shard_map/ppermute | solution.py:27
  504.7 30.9 %collective-permute-start.7 = (bf16[160,2048]{1,0:T(8,128)(2,1)S(1)}, bf16[160,2048]{1,0:T(8,128)(2,1)S(1)}, u32[]{:S(2)}, u32[]{:S(2)}) collective-permute-start(bf16[160,2048]{1,0:T(8,128)(2,1)S(1)} %get-tuple-element.61), channel_id=1, source_target_pairs={{0,3},{1,0},{2,1},{3,2},{4,7},{5,4},{6,5},{7,6},{8,11},{9,8},{10,9... | collective-permute-start | bytes 1966088 | tf_op jit(solution)/shard_map/ppermute | solution.py:32
  523.5 26.7 %collective-permute-start.8 = (bf16[160,2048]{1,0:T(8,128)(2,1)S(1)}, bf16[160,2048]{1,0:T(8,128)(2,1)S(1)}, u32[]{:S(2)}, u32[]{:S(2)}) collective-permute-start(bf16[160,2048]{1,0:T(8,128)(2,1)S(1)} %collective-permute-done.6), channel_id=1, source_target_pairs={{0,1},{1,2},{2,3},{3,0},{4,5},{5,6},{6,7},{7,4},{8,9},{9,10},{10,1... | collective-permute-start | bytes 1966088 | tf_op jit(solution)/shard_map/ppermute | solution.py:27
  594.6 50.7 %copy-start.23 = (bf16[4,20,8,512]{3,2,0,1:T(8,128)(2,1)S(1)}, bf16[4,20,8,512]{3,2,0,1:T(8,128)(2,1)}, u32[]{:S(2)}) copy-start(bf16[4,20,8,512]{3,2,0,1:T(8,128)(2,1)} %copy-done.21) | copy-start | bytes 1966084
  594.6 50.7 %copy-start.25 = (bf16[160,2048]{1,0:T(8,128)(2,1)S(1)}, bf16[160,2048]{1,0:T(8,128)(2,1)}, u32[]{:S(2)}) copy-start(bf16[160,2048]{1,0:T(8,128)(2,1)} %reduce-scatter.9.cloned.1.call-done) | copy-start | bytes 1966084
  594.6 50.7 %copy-start.27 = (bf16[160,2048]{1,0:T(8,128)(2,1)S(1)}, bf16[160,2048]{1,0:T(8,128)(2,1)}, u32[]{:S(2)}) copy-start(bf16[160,2048]{1,0:T(8,128)(2,1)} %reduce-scatter.7.cloned.1.call-done) | copy-start | bytes 1966084
  648.8 19.5 %collective-permute-start.9 = (bf16[160,2048]{1,0:T(8,128)(2,1)S(1)}, bf16[160,2048]{1,0:T(8,128)(2,1)S(1)}, u32[]{:S(2)}, u32[]{:S(2)}) collective-permute-start(bf16[160,2048]{1,0:T(8,128)(2,1)S(1)} %get-tuple-element.59), channel_id=1, source_target_pairs={{0,1},{1,2},{2,3},{3,0},{4,5},{5,6},{6,7},{7,4},{8,9},{9,10},{10,1... | collective-permute-start | bytes 1966088 | tf_op jit(solution)/shard_map/ppermute | solution.py:27
  649.5 30.9 %collective-permute-start.10 = (bf16[160,2048]{1,0:T(8,128)(2,1)S(1)}, bf16[160,2048]{1,0:T(8,128)(2,1)S(1)}, u32[]{:S(2)}, u32[]{:S(2)}) collective-permute-start(bf16[160,2048]{1,0:T(8,128)(2,1)S(1)} %get-tuple-element.59), channel_id=1, source_target_pairs={{0,3},{1,0},{2,1},{3,2},{4,7},{5,4},{6,5},{7,6},{8,11},{9,8},{10,9... | collective-permute-start | bytes 1966088 | tf_op jit(solution)/shard_map/ppermute | solution.py:32
  668.3 26.8 %collective-permute-start.11 = (bf16[160,2048]{1,0:T(8,128)(2,1)S(1)}, bf16[160,2048]{1,0:T(8,128)(2,1)S(1)}, u32[]{:S(2)}, u32[]{:S(2)}) collective-permute-start(bf16[160,2048]{1,0:T(8,128)(2,1)S(1)} %collective-permute-done.9), channel_id=1, source_target_pairs={{0,1},{1,2},{2,3},{3,0},{4,5},{5,6},{6,7},{7,4},{8,9},{9,10},{10,1... | collective-permute-start | bytes 1966088 | tf_op jit(solution)/shard_map/ppermute | solution.py:27
  680.4 18.1 %copy-start.39 = (bf16[512,2048]{1,0:T(8,128)(2,1)S(1)}, bf16[512,2048]{1,0:T(8,128)(2,1)}, u32[]{:S(2)}) copy-start(bf16[512,2048]{1,0:T(8,128)(2,1)} %all-gather.9.cloned.1.call-done) | copy-start | bytes 6291460
  789.2 28.0 %all-to-all-start.6 = ((bf16[4,640,384]{2,1,0:T(8,128)(2,1)}), bf16[4,640,384]{2,1,0:T(8,128)(2,1)S(1)}, u32[]{:S(2)}, u32[]{:S(2)}) async-start(bf16[4,640,384]{2,1,0:T(8,128)(2,1)} %bitcast.237), calls=%async_computation.9 | async-start | bytes 3932160 | tf_op jit(solution)/shard_map/all_to_all | solution.py:195
  792.9 77.3 %reduce-scatter.15.cloned.1.call-start = ((), (), s32[]{:S(2)}) async-start(), calls=%async_computation.21 | async-start | bytes 573440 | tf_op jit(solution)/shard_map/reduce_scatter | solution.py:305
  829.7 19.8 %copy-start.67 = (bf16[640,16]{0,1:T(8,128)(2,1)}, bf16[640,16]{0,1:T(8,128)(2,1)S(1)}, u32[]{:S(2)}) copy-start(bf16[640,16]{0,1:T(8,128)(2,1)S(1)} %convolution_convert_fusion.10) | copy-start | bytes 61444
  851.0 54.4 %all-reduce.7.cloned.1.call-start = ((), (), s32[]{:S(2)}) async-start(), calls=%async_computation.23 | async-start | bytes 524288
  859.8 82.5 %all-reduce.5.cloned.1.call-start = ((), (), s32[]{:S(2)}) async-start(), calls=%async_computation.22 | async-start | bytes 229376
  871.8 125.0 %reduce-scatter.13.cloned.1.call-start = ((), (), s32[]{:S(2)}) async-start(), calls=%async_computation.20 | async-start | bytes 3276800 | tf_op jit(solution)/shard_map/reduce_scatter | solution.py:172
  878.7 14.3 %all-to-all-start.3 = ((bf16[160,4,512]{2,0,1:T(8,128)(2,1)}), bf16[160,4,512]{2,0,1:T(8,128)(2,1)S(1)}, u32[]{:S(2)}, u32[]{:S(2)}) async-start(bf16[160,4,512]{2,0,1:T(8,128)(2,1)} %bitcast.209), calls=%async_computation.5 | async-start | bytes 1310720 | tf_op jit(solution)/shard_map/all_to_all | solution.py:166
  949.3 47.5 %copy-start.4 = (f32[4,20,8,512]{3,2,0,1:T(8,128)S(1)}, f32[4,20,8,512]{3,2,0,1:T(8,128)}, u32[]{:S(2)}) copy-start(f32[4,20,8,512]{3,2,0,1:T(8,128)} %copy-done.3) | copy-start | bytes 3932164
  949.3 47.5 %copy-start.29 = (bf16[160,2048]{1,0:T(8,128)(2,1)S(1)}, bf16[160,2048]{1,0:T(8,128)(2,1)}, u32[]{:S(2)}) copy-start(bf16[160,2048]{1,0:T(8,128)(2,1)} %reduce-scatter.11.cloned.1.call-done) | copy-start | bytes 1966084
  954.0 45.1 %copy-start.43 = (f32[4,7,4,512]{3,2,1,0:T(4,128)}, f32[4,7,4,512]{3,2,1,0:T(4,128)S(1)}, u32[]{:S(2)}) copy-start(f32[4,7,4,512]{3,2,1,0:T(4,128)S(1)} %reshape.348) | copy-start | bytes 688132
  999.1 15.9 %copy-start.1 = (f32[2,8,16,2048]{3,2,1,0:T(8,128)S(1)}, f32[2,8,16,2048]{3,2,1,0:T(8,128)}, u32[]{:S(2)}) copy-start(f32[2,8,16,2048]{3,2,1,0:T(8,128)} %param.41) | copy-start | bytes 6291460
  999.1 13.8 %all-to-all-start.7 = ((bf16[160,4,512]{2,0,1:T(8,128)(2,1)}), bf16[160,4,512]{2,0,1:T(8,128)(2,1)S(1)}, u32[]{:S(2)}, u32[]{:S(2)}) async-start(bf16[160,4,512]{2,0,1:T(8,128)(2,1)} %bitcast.208), calls=%async_computation.11 | async-start | bytes 1310720 | tf_op jit(solution)/shard_map/all_to_all | solution.py:166
  (68 other events, 325.8 us)
Sparse Core Ops, SparseCore 0:
  10.1 52.1 all-gather.6
  130.1 32.6 all-gather.8
  220.8 49.3 reduce-scatter.6
  271.7 105.5 all-gather.10
  378.7 58.2 all-gather.12
  448.3 52.0 reduce-scatter.8
  594.7 50.4 reduce-scatter.10
  851.1 19.0 reduce-scatter.14
  873.2 32.1 all-reduce.6
  908.3 34.0 all-reduce.4
  944.7 52.0 reduce-scatter.12
